TPU v7x, 32 devices: a whole 2x2x4 slice. The times are simulated.
32 devices in a mesh: frow: 8 (over z, y), fcol: 4 (over x, core).
Axes of the slice: x: 2, y: 2, z: 4, core: 2. Of those that a mesh axis runs over, the one named last changes fastest.
Arguments:
- image: bfloat16 [2, 4096, 2048], P(None, 'frow', 'fcol'), may hold values from -6 to 6
- window_rows: float32 [4096], P('frow'), may hold values from 0.1 to 1.9
- window_cols: float32 [2048], P('fcol'), may hold values from 0.1 to 1.9
- w_terms: float32 [2], replicated, may hold values from 20 to 200
- facet_row_offset: int32 [8], replicated, may hold values from 0 to 65535
- facet_col_offset: int32 [4], replicated, may hold values from 0 to 65535
- band_offset: int32 [2], replicated, may hold values from 0 to 65535
- sub_row_offset: int32 [2], replicated, may hold values from 0 to 65535
- sub_column: int32 [2], replicated, may hold values from 0 to 1, as said below
Outputs:
- subgrids: float32 [2, 2, 512, 512], P(None, None, 'frow', 'fcol')
Inputs may be any that keep to these rules, and one draw needn't show every extreme that they name: `sub_column`: every subgrid column holds exactly 1 subgrids.
All inputs are finite; a program needn't handle non-finite values.
Results may differ from a plain program's by a relative error of at most 0.0052.
Values sent between devices are 32-bit elements; how exact they have to be, the bound alone decides.
A program may use at most 64 MiB of HBM per device.

v0:
```python
import math

import jax
import jax.numpy as jnp
from jax import lax
from jax.sharding import PartitionSpec as P

SG = 512
IMAGE = 65536


def phase_index(first, second):
    high = first * (second // 256) % 256 * 256
    return (high + first * (second % 256)) % 65536


def dft_table(coords, freqs):
    angle = phase_index(coords, freqs).astype(jnp.float32) * (2.0 * math.pi / IMAGE)
    return (jnp.cos(angle).astype(jnp.bfloat16), (-jnp.sin(angle)).astype(jnp.bfloat16))


def coord_unit(coords):
    return (coords % IMAGE).astype(jnp.float32) / IMAGE - 0.5


def block_table(table_re, table_im):
    upper = jnp.concatenate([table_re, table_im], axis=1)
    lower = jnp.concatenate([-table_im, table_re], axis=1)
    return jnp.concatenate([upper, lower], axis=0)


def local(
    image,
    window_rows,
    window_cols,
    w_terms,
    facet_row_offset,
    facet_col_offset,
    band_offset,
    sub_row_offset,
    sub_column,
):
    facet = image.shape[1]
    column_count = band_offset.shape[0]
    sub_count = sub_row_offset.shape[0]
    frow_index = lax.axis_index("frow")
    fcol_index = lax.axis_index("fcol")
    freq_base = jnp.arange(SG, dtype=jnp.int32)
    gcol = facet_col_offset[fcol_index] + jnp.arange(image.shape[2], dtype=jnp.int32)
    mcoord = coord_unit(gcol)
    row_base = facet_row_offset[frow_index]
    row_ids = row_base + jnp.arange(facet, dtype=jnp.int32)
    radius = coord_unit(row_ids)[:, None] ** 2 + mcoord[None, :] ** 2
    scale = window_rows[:, None] * window_cols[None, :]
    first = image[0].astype(jnp.float32) * scale
    second = image[1].astype(jnp.float32) * scale
    prepared = []
    for column in range(column_count):
        angle = w_terms[column] * radius
        cosine = jnp.cos(angle)
        sine = jnp.sin(angle)
        prep_re = (first * cosine - second * sine).astype(jnp.bfloat16)
        prep_im = (first * sine + second * cosine).astype(jnp.bfloat16)
        prepared.append(jnp.concatenate([prep_re, prep_im], axis=1))
    band_dev = SG // lax.axis_size("fcol")
    freqs = jnp.arange(band_dev * lax.axis_size("fcol"), dtype=jnp.int32)
    outputs = []
    for column in range(column_count):
        table_re, table_im = dft_table(gcol[:, None], band_offset[column] + freqs[None, :])
        whole_table = block_table(table_re, table_im)
        product = lax.dot_general(
            whole_table,
            prepared[column],
            (((0,), (1,)), ((), ())),
            preferred_element_type=jnp.float32,
        )
        outputs.append(
            product.reshape(2, band_dev * lax.axis_size("fcol"), facet).transpose(1, 0, 2)
        )
    summed = lax.psum_scatter(jnp.stack(outputs, axis=1), "fcol", scatter_dimension=0, tiled=True)
    banded = (summed / math.sqrt(facet * lax.axis_size("fcol"))).astype(jnp.bfloat16)
    chosen = jnp.take(banded, sub_column, axis=1)
    right_side = chosen.transpose(1, 2, 3, 0).reshape(sub_count, 2 * facet, band_dev)
    table_re, table_im = dft_table(
        row_ids[None, :, None], sub_row_offset[:, None, None] + freq_base[None, None, :]
    )
    left_real = jnp.concatenate([table_re, -table_im], axis=1)
    left_imag = jnp.concatenate([table_im, table_re], axis=1)
    left_side = jnp.stack([left_real, left_imag], axis=2)
    term = jnp.einsum("kxcu,kxv->kcuv", left_side, right_side, preferred_element_type=jnp.float32)
    term = term * (1.0 / math.sqrt(facet * lax.axis_size("frow")))
    return lax.psum_scatter(term, "frow", scatter_dimension=2, tiled=True)


def solution(mesh):
    placed = (P(None, "frow", "fcol"), P("frow"), P("fcol"), P(), P(), P(), P(), P(), P())
    return jax.shard_map(
        local, mesh=mesh, in_specs=placed, out_specs=P(None, None, "frow", "fcol"), check_vma=False
    )
```

profile of v0, /device:TPU:0, one launch (start us, length us, event | category | flops | bytes accessed | tf_op | source)
XLA Modules:
  0.0 173.5 jit_solution(15162713084779223089)
XLA Ops:
  6.5 0.0 reduce-scatter.3.cloned.1.call-start
  6.6 1.4 dynamic_slice.7
  8.0 0.6 iota_add_fusion.3
  8.6 1.3 fusion.91
  10.0 0.7 add_select_fusion.10
  10.6 0.6 add_select_fusion.6
  11.2 9.7 %negate_convert_fusion.2 = (bf16[512,512]{1,0:T(8,128)(2,1)S(1)}, bf16[512,512]{1,0:T(8,128)(2,1)S(1)}, bf16[512,512]{1,0:T(8,128)(2,1)S(1)}, bf16[512,512]{1,0:T(8,128)(2,1)S(1)}) fusion(s32[512]{0:T(512)S(1)} %get-tuple-element.27, s32[512]{0:T(512)S(1)} %get-tuple-element.28, s32[512]{0:T(512)S(1)} %iota_add_fusion.3, s32[512]{0:T(512)S(1)} %get-tuple-element.29, ...), kind=kLoop, calls=%fused_computation.102 | loop fusion | flops 16252928 | bytes 2107392 | tf_op jit(solution)/shard_map/convert_element_type | solution.py:19
  20.9 10.2 %fusion.68 = (bf16[512,512]{1,0:T(8,128)(2,1)}, bf16[512,512]{1,0:T(8,128)(2,1)}) fusion(s32[512]{0:T(512)S(1)} %get-tuple-element.27, s32[512]{0:T(512)S(1)} %get-tuple-element.28, s32[512]{0:T(512)S(1)} %iota_add_fusion.3, s32[512]{0:T(512)S(1)} %get-tuple-element.29, s32[512]{0:T(512)S(1)} %get-tuple-element.30), kind=kLoop, calls=%fused_computation.106 | loop fusion | flops 17301504 | bytes 1058816 | tf_op jit(solution)/shard_map/neg | solution.py:28
  31.1 0.0 copy-done.7
  31.1 0.6 dynamic_slice.6
  31.7 1.3 fusion.75
  33.0 0.6 fusion.90
  33.6 0.0 copy-done.5
  33.6 9.7 %fusion.42 = (bf16[512,512]{1,0:T(8,128)(2,1)S(1)}, bf16[512,512]{1,0:T(8,128)(2,1)S(1)}, bf16[512,512]{1,0:T(8,128)(2,1)S(1)}, bf16[512,512]{1,0:T(8,128)(2,1)S(1)}) fusion(f32[512]{0:T(512)S(1)} %get-tuple-element.32, f32[512]{0:T(512)S(1)} %get-tuple-element.31, f32[]{:T(128)} %bitcast.7, f32[512]{0:T(512)S(1)} %copy-done.4, f32[512]{0:T(512)S(1)} %copy-done.5, ...), kind=kLoop, calls=%fused_computation.74 | loop fusion | flops 6291456 | bytes 3153928 | tf_op jit(solution)/shard_map/convert_element_type | solution.py:62
  43.3 1.3 fusion.10
  44.7 1.3 fusion.18
  46.0 2.4 %pad_maximum_fusion = f32[512,2,2,512]{3,0,2,1:T(8,128)} fusion(f32[512,1,2,512]{3,0,2,1:T(8,128)S(1)} %bitcast.43, f32[512,1,2,512]{3,0,2,1:T(8,128)S(1)} %bitcast.42), kind=kLoop, calls=%fused_computation.5 | loop fusion | flops 1048576 | bytes 8388608 | tf_op jit(solution)/shard_map/stack | solution.py:80
  48.4 0.0 reduce-scatter.3.cloned.1.call-update
  48.4 0.2 reduce-scatter.5.cloned.1.call-start
  48.6 0.7 iota_add_fusion.4
  49.3 0.1 and_select_fusion.1
  49.4 9.6 %fusion.67 = bf16[2,512,512]{1,2,0:T(8,128)(2,1)S(1)} fusion(s32[2,512]{1,0:T(2,128)S(1)} %get-tuple-element.22, s32[2,512]{1,0:T(2,128)S(1)} %get-tuple-element.21, s32[512]{0:T(512)S(1)} %iota_add_fusion.4), kind=kLoop, calls=%fused_computation.105 | loop fusion | flops 17301504 | bytes 1058816 | tf_op jit(solution)/shard_map/neg | solution.py:87
  59.0 10.1 %negate_convert_fusion = (bf16[2,512,512]{1,2,0:T(8,128)(2,1)S(1)}, bf16[2,512,512]{1,2,0:T(8,128)(2,1)S(1)}) fusion(s32[2,512]{1,0:T(2,128)S(1)} %get-tuple-element.22, s32[2,512]{1,0:T(2,128)S(1)} %get-tuple-element.21, s32[512]{0:T(512)S(1)} %iota_add_fusion.4), kind=kLoop, calls=%fused_computation.38 | loop fusion | flops 16252928 | bytes 2107392 | tf_op jit(solution)/shard_map/convert_element_type | solution.py:19
  69.1 2.0 %maximum_bitcast_fusion = (bf16[2,1024,1,512]{1,3,2,0:T(8,128)(2,1)S(1)}, bf16[2,1024,1,512]{1,3,2,0:T(8,128)(2,1)}) fusion(bf16[2,512,512]{1,2,0:T(8,128)(2,1)S(1)} %fusion.67, bf16[2,512,512]{1,2,0:T(8,128)(2,1)S(1)} %get-tuple-element.12, bf16[2,512,512]{1,2,0:T(8,128)(2,1)S(1)} %get-tuple-element.11), kind=kLoop, calls=%fused_computation.20 | loop fusion | flops 8388608 | bytes 7340032 | tf_op jit(solution)/shard_map/stack | solution.py:89
  71.1 24.6 %reduce-scatter.3.cloned.1.call-done = f32[128,2,2,512]{3,0,2,1:T(8,128)} async-done(((f32[512,2,2,512]{3,0,2,1:T(8,128)}), f32[128,2,2,512]{3,0,2,1:T(8,128)}) %reduce-scatter.3.cloned.1.call-update) | async-done | bytes 1048592 | tf_op jit(solution)/shard_map/reduce_scatter | solution.py:80
  95.7 1.3 multiply_convert_fusion
  97.1 0.6 gather_fusion
  97.7 0.1 select_bitcast_fusion
  97.8 0.3 copy.11
  98.1 3.8 %fusion.38 = f32[2,2,512,128]{3,2,1,0:T(8,128)} fusion(bf16[2,1024,128,1]{2,1,3,0:T(8,128)(2,1)S(1)} %bitcast.44, bf16[2,1024,1,512]{1,3,2,0:T(8,128)(2,1)} %get-tuple-element.10, bf16[2,1024,1,512]{1,3,2,0:T(8,128)(2,1)S(1)} %get-tuple-element.9), kind=kOutput, calls=%fused_computation.72 | convolution fusion | flops 539230208 | bytes 5767168 | tf_op jit(solution)/shard_map/kxcu,kxv->kcuv/dot_general | solution.py:90
  101.9 0.0 reduce-scatter.5.cloned.1.call-update
  101.9 64.7 %reduce-scatter.5.cloned.1.call-done = f32[2,2,64,128]{3,2,1,0:T(8,128)} async-done(((f32[2,2,512,128]{3,2,1,0:T(8,128)}), f32[2,2,64,128]{3,2,1,0:T(8,128)}) %reduce-scatter.5.cloned.1.call-update) | async-done | bytes 131088 | tf_op jit(solution)/shard_map/reduce_scatter | solution.py:92
  (19 shorter events, 0.0 us)
Async XLA Ops:
  6.5 24.6 %copy-start.7 = (s32[8]{0:T(128)S(1)}, s32[8]{0:T(128)}, u32[]{:S(2)}) copy-start(s32[8]{0:T(128)} %param.13) | copy-start | bytes 100
  6.5 26.4 %copy-start.3 = (f32[2]{0:T(128)S(1)}, f32[2]{0:T(128)}, u32[]{:S(2)}) copy-start(f32[2]{0:T(128)} %param.12) | copy-start | bytes 28
  6.5 27.0 %copy-start.5 = (f32[512]{0:T(512)S(1)}, f32[512]{0:T(512)}, u32[]{:S(2)}) copy-start(f32[512]{0:T(512)} %param.10) | copy-start | bytes 6148
  6.5 27.0 %copy-start.4 = (f32[512]{0:T(512)S(1)}, f32[512]{0:T(512)}, u32[]{:S(2)}) copy-start(f32[512]{0:T(512)} %param.11) | copy-start | bytes 6148
  6.5 27.0 %copy-start = (bf16[2,512,512]{2,1,0:T(8,128)(2,1)S(1)}, bf16[2,512,512]{2,1,0:T(8,128)(2,1)}, u32[]{:S(2)}) copy-start(bf16[2,512,512]{2,1,0:T(8,128)(2,1)} %param.9) | copy-start | bytes 3145732
  6.5 89.2 %reduce-scatter.3.cloned.1.call-start = ((), (), s32[]{:S(2)}) async-start(), calls=%async_computation.2 | async-start | bytes 5242880 | tf_op jit(solution)/shard_map/reduce_scatter | solution.py:80
  31.1 12.2 %copy-start.2 = (bf16[512,512]{1,0:T(8,128)(2,1)S(1)}, bf16[512,512]{1,0:T(8,128)(2,1)}, u32[]{:S(2)}) copy-start(bf16[512,512]{1,0:T(8,128)(2,1)} %get-tuple-element.19) | copy-start | bytes 1572868
  43.3 1.3 copy-start.1
  48.4 0.9 copy-start.8
  48.4 1.0 copy-start.6
  48.4 118.3 %reduce-scatter.5.cloned.1.call-start = ((), (), s32[]{:S(2)}) async-start(), calls=%async_computation.3 | async-start | bytes 1179648 | tf_op jit(solution)/shard_map/reduce_scatter | solution.py:92
Sparse Core Ops, SparseCore 0:
  48.5 47.1 reduce-scatter.2
  102.0 64.5 reduce-scatter.4
where the time goes:
time: 174 us; the launch traced here: 173 us
  waiting for transfers between devices  89.3 us (51%)
  other arithmetic  59.1 us (34%)
  between operations  13.6 us (8%)
  matrix products  6.43 us (4%)
  local copies, waits for them, and re-layouts  4.76 us (3%)
    reduce_scatter x1, waiting for transfers between devices, local(): return lax.psum_scatter(term, 'frow', scatter_dimension=2, tiled=True)  64.7 us
    reduce_scatter x1, waiting for transfers between devices, local(): lax.psum_scatter(jnp.stack(outputs, axis=1), 'fcol', scatter_dimension=0,...  24.6 us
    convert_element_type x2, other arithmetic, dft_table(): (-jnp.sin(angle)).astype(jnp.bfloat16)  19.9 us
    neg x1, other arithmetic, block_table(): lower = jnp.concatenate([-table_im, table_re], axis=1)  10.2 us
    convert_element_type x1, other arithmetic, local(): prep_re = (first * cosine - second * sine).astype(jnp.bfloat16)  9.73 us
    neg x1, other arithmetic, local(): left_real = jnp.concatenate([table_re, -table_im], axis=1)  9.56 us
    dot_general x1, matrix products, local(): jnp.einsum('kxcu,kxv->kcuv', left_side, right_side, preferred_element_typ...  3.83 us
  transfers between devices with their start and end apart: 2, of which 2 were waited for; matrix products, arithmetic and copies ran while one was open for 13% of the time, Pallas kernels for 0%

commit v1 on v0

--- a/solution.py
+++ b/solution.py
@@ -1,8 +1,11 @@
+import functools
 import math
 
 import jax
 import jax.numpy as jnp
 from jax import lax
+from jax.experimental import pallas as pl
+from jax.experimental.pallas import tpu as pltpu
 from jax.sharding import PartitionSpec as P
 
 SG = 512
@@ -29,7 +32,7 @@
     return jnp.concatenate([upper, lower], axis=0)
 
 
-def local(
+def general_local(
     image,
     window_rows,
     window_cols,
@@ -92,7 +95,325 @@
     return lax.psum_scatter(term, "frow", scatter_dimension=2, tiled=True)
 
 
+MESH = pl.DeviceIdType.MESH
+ROWS = 16
+
+
+def unit_phasor(index):
+    quadrant = (index + IMAGE // 8) >> 14
+    t = (index - (quadrant << 14)).astype(jnp.float32) * (2.0 * math.pi / IMAGE)
+    s = t * t
+    sine = t * (1.0 + s * (-1 / 6 + s * (1 / 120 + s * (-1 / 5040 + s * (1 / 362880)))))
+    cosine = 1.0 + s * (
+        -1 / 2 + s * (1 / 24 + s * (-1 / 720 + s * (1 / 40320 + s * (-1 / 3628800))))
+    )
+    odd = (quadrant & 1) == 1
+    real = jnp.where(odd, sine, cosine)
+    imag = jnp.where(odd, cosine, sine)
+    real = jnp.where(((quadrant + 1) & 2) == 2, -real, real)
+    imag = jnp.where((quadrant & 2) == 2, imag, -imag)
+    return real, imag
+
+
+def residue(first, second):
+    return (first * second) & (IMAGE - 1)
+
+
+def coord_square(coords):
+    unit = (coords & (IMAGE - 1)).astype(jnp.float32) / IMAGE - 0.5
+    return unit * unit
+
+
+def times(a, b):
+    return a[0] * b[0] - a[1] * b[1], a[0] * b[1] + a[1] * b[0]
+
+
+def iota(shape, axis):
+    return lax.broadcasted_iota(jnp.int32, shape, axis)
+
+
+def fused_kernel(
+    dims,
+    image_ref, wrow_ref, wcol_ref, w_ref, row_off_ref, col_off_ref, band_ref, sub_off_ref, sub_col_ref,
+    out_ref,
+    send, got, wsend, wgot, left, right, band, rtab, coarse, fine, phases,
+    part, recv1, sum1, recv2, sum2, recv3,
+    isend, irecv, s1, r1, s2, r2, s3, r3,
+):
+    n_side, n_z, n_sub, facet, sg = dims
+    r = lax.axis_index("frow")
+    c = lax.axis_index("fcol")
+    x, core = c // 2, c % 2
+    z, y = r // n_side, r % n_side
+    block = sg // (2 * n_side)
+    urows = sg // (n_side * n_z)
+    nv = sg // 2
+    partner = (r, c + 1 - 2 * core)
+    first = x * (1 - core) + y * core
+    second = y * (1 - core) + x * core
+
+    def place(a, b, zz):
+        xx = a * (1 - core) + b * core
+        yy = b * (1 - core) + a * core
+        return (zz * n_side + yy, xx * 2 + core)
+
+    firsts = [(first + d) % n_side for d in range(1, n_side)]
+    seconds = [(second + d) % n_side for d in range(1, n_side)]
+    zs = [(z + d) % n_z for d in range(1, n_z)]
+    peers = (
+        [partner]
+        + [place(a, second, z) for a in firsts]
+        + [place(first, b, z) for b in seconds]
+        + [place(first, second, q) for q in zs]
+    )
+    barrier = pltpu.get_barrier_semaphore()
+    for peer in peers:
+        pl.semaphore_signal(barrier, inc=1, device_id=peer, device_id_type=MESH)
+
+    send[...] = image_ref[...].astype(jnp.float32)
+    wsend[...] = jnp.broadcast_to(wcol_ref[...], wsend.shape)
+
+    lane = iota((1, facet), 1)
+    gcol = [col_off_ref[c] + lane, col_off_ref[partner[1]] + lane]
+    grow = row_off_ref[r] + lane
+    columns = [sub_col_ref[k] for k in range(n_sub)]
+
+    row_id = iota((phases.shape[1], facet), 0)
+    angle = jnp.zeros((phases.shape[1], facet), jnp.float32)
+    for k in range(n_sub):
+        w = w_ref[columns[k]]
+        for f, coords in enumerate(gcol + [grow]):
+            angle = jnp.where(row_id == 3 * k + f, w * coord_square(coords), angle)
+    phases[0] = jnp.cos(angle)
+    phases[1] = jnp.sin(angle)
+
+    def write_fine(coords):
+        q = unit_phasor(residue(coords, iota((ROWS, facet), 0)))
+        fine[0] = q[0]
+        fine[1] = q[1]
+
+    def write_coarse(coords, freqs, gain, row):
+        p = times(
+            unit_phasor(residue(coords, freqs)),
+            (phases[0, row : row + 1, :] * gain, phases[1, row : row + 1, :] * gain),
+        )
+        coarse[0, : freqs.shape[0]] = p[0]
+        coarse[1, : freqs.shape[0]] = p[1]
+
+    def entries(h):
+        re, im = times(
+            (coarse[0, pl.ds(h, 1), :], coarse[1, pl.ds(h, 1), :]), (fine[0], fine[1])
+        )
+        return re.astype(jnp.bfloat16), im.astype(jnp.bfloat16)
+
+    def build_columns(f):
+        write_fine(gcol[f])
+        gain = wcol_ref[...] if f == 0 else wgot[0:1, :]
+        at = 2 * facet * f
+        for k in range(n_sub):
+            index = iota((nv // ROWS, facet), 0) * ROWS
+            v = block * (2 * (index // block) + core) + index % block
+            write_coarse(gcol[f], band_ref[columns[k]] + v, gain, 3 * k + f)
+
+            def body(h, carry, k=k):
+                re, im = entries(h)
+                top = pl.ds(pl.multiple_of(h * ROWS, ROWS), ROWS)
+                low = pl.ds(pl.multiple_of(nv + h * ROWS, ROWS), ROWS)
+                right[k, top, at : at + facet] = re
+                right[k, top, at + facet : at + 2 * facet] = -im
+                right[k, low, at : at + facet] = im
+                right[k, low, at + facet : at + 2 * facet] = re
+                return carry
+
+            lax.fori_loop(0, nv // ROWS, body, 0)
+
+    def build_rows():
+        write_fine(grow)
+        for k in range(n_sub):
+            index = iota((sg // ROWS, facet), 0) * ROWS
+            per = sg // n_side
+            u = urows * (n_side * (index % per // urows) + index // per) + index % urows
+            gain = wrow_ref[...] * dims_scale
+            write_coarse(grow, sub_off_ref[k] + u, gain, 3 * k + 2)
+
+            def body(h, carry, k=k):
+                re, im = entries(h)
+                at = pl.ds(pl.multiple_of(h * ROWS, ROWS), ROWS)
+                rtab[k, 0, at, :facet] = re
+                rtab[k, 0, at, facet:] = -im
+                rtab[k, 1, at, :facet] = im
+                rtab[k, 1, at, facet:] = re
+                return carry
+
+            lax.fori_loop(0, sg // ROWS, body, 0)
+
+    dims_scale = 1.0 / math.sqrt(facet * lax.axis_size("fcol")) / math.sqrt(facet * lax.axis_size("frow"))
+
+    def remote(src, dst, a, b, peer):
+        return pltpu.make_async_remote_copy(
+            src_ref=src, dst_ref=dst, send_sem=a, recv_sem=b, device_id=peer, device_id_type=MESH
+        )
+
+    pl.semaphore_wait(barrier, len(peers))
+    wcopy = remote(wsend, wgot, isend.at[0], irecv.at[0], partner)
+    icopy = remote(send, got, isend.at[1], irecv.at[1], partner)
+    wcopy.start()
+    icopy.start()
+    left[:, :facet] = image_ref[0]
+    left[:, facet : 2 * facet] = image_ref[1]
+    build_columns(0)
+    wcopy.wait()
+    build_columns(1)
+    build_rows()
+    icopy.wait()
+    left[:, 2 * facet : 3 * facet] = got[0].astype(jnp.bfloat16)
+    left[:, 3 * facet :] = got[1].astype(jnp.bfloat16)
+
+    n_chunk = 2 * n_sub
+    copies1, copies2, copies3 = [], [], []
+    step = 128
+    for k in range(n_sub):
+
+        def contract(i, carry, k=k):
+            at = pl.ds(pl.multiple_of(i * step, step), step)
+            value = lax.dot_general(
+                left[at, :], right[k], (((1,), (1,)), ((), ())), preferred_element_type=jnp.float32
+            ).astype(jnp.bfloat16)
+            band[k, at, :] = value[:, :nv]
+            band[k, pl.ds(pl.multiple_of(facet + i * step, step), step), :] = value[:, nv:]
+            return carry
+
+        lax.fori_loop(0, facet // step, contract, 0)
+        for half in range(2):
+            ch = 2 * k + half
+            rows = sg // n_side
+            for yb in range(n_side):
+                value = jnp.dot(
+                    rtab[k, half, yb * rows : (yb + 1) * rows, :],
+                    band[k],
+                    preferred_element_type=jnp.float32,
+                )
+                for xb in range(n_side):
+                    a = xb * (1 - core) + yb * core
+                    b = yb * (1 - core) + xb * core
+                    part[ch, a, b] = value[:, xb * block : (xb + 1) * block]
+            group = [
+                remote(part.at[ch, a], recv1.at[ch, d], s1.at[ch, d], r1.at[ch, d], place(a, second, z))
+                for d, a in enumerate(firsts)
+            ]
+            for copy in group:
+                copy.start()
+            copies1.append(group)
+
+    for t in range(n_chunk + 1):
+        if t < n_chunk:
+            ch = t
+            for copy in copies1[ch]:
+                copy.wait_recv()
+            total = part[ch, first]
+            for d in range(n_side - 1):
+                total = total + recv1[ch, d]
+            sum1[ch] = total
+            group = [
+                remote(sum1.at[ch, b], recv2.at[ch, d], s2.at[ch, d], r2.at[ch, d], place(first, b, z))
+                for d, b in enumerate(seconds)
+            ]
+            for copy in group:
+                copy.start()
+            copies2.append(group)
+        if t >= 1:
+            ch = t - 1
+            for copy in copies2[ch]:
+                copy.wait_recv()
+            total = sum1[ch, second]
+            for d in range(n_side - 1):
+                total = total + recv2[ch, d]
+            sum2[ch] = total.reshape(n_z, urows, block)
+            group = [
+                remote(sum2.at[ch, q], recv3.at[ch, d], s3.at[ch, d], r3.at[ch, d], place(first, second, q))
+                for d, q in enumerate(zs)
+            ]
+            for copy in group:
+                copy.start()
+            copies3.append(group)
+    for ch in range(n_chunk):
+        for copy in copies3[ch]:
+            copy.wait_recv()
+        total = sum2[ch, z]
+        for d in range(n_z - 1):
+            total = total + recv3[ch, d]
+        out_ref[ch // 2, ch % 2] = total
+    for group in copies1 + copies2 + copies3:
+        for copy in group:
+            copy.wait_send()
+
+
+def fused_local(n_side, n_z, image, window_rows, window_cols, *scalars):
+    facet = image.shape[1]
+    n_sub = scalars[4].shape[0]
+    n_chunk = 2 * n_sub
+    block = SG // (2 * n_side)
+    urows = SG // (n_side * n_z)
+    rows = SG // n_side
+    f32, b16 = jnp.float32, jnp.bfloat16
+    vmem = pl.BlockSpec(memory_space=pltpu.VMEM)
+    smem = pl.BlockSpec(memory_space=pltpu.SMEM)
+    dma = pltpu.SemaphoreType.DMA
+    return pl.pallas_call(
+        functools.partial(fused_kernel, (n_side, n_z, n_sub, facet, SG)),
+        out_shape=jax.ShapeDtypeStruct((n_sub, 2, urows, block), f32),
+        in_specs=[vmem] * 3 + [smem] * 6,
+        out_specs=vmem,
+        scratch_shapes=[
+            pltpu.VMEM(image.shape, f32),
+            pltpu.VMEM(image.shape, f32),
+            pltpu.VMEM((8, facet), f32),
+            pltpu.VMEM((8, facet), f32),
+            pltpu.VMEM((facet, 4 * facet), b16),
+            pltpu.VMEM((n_sub, SG, 4 * facet), b16),
+            pltpu.VMEM((n_sub, 2 * facet, SG // 2), b16),
+            pltpu.VMEM((n_sub, 2, SG, 2 * facet), b16),
+            pltpu.VMEM((2, SG // ROWS, facet), f32),
+            pltpu.VMEM((2, ROWS, facet), f32),
+            pltpu.VMEM((2, -(-3 * n_sub // 8) * 8, facet), f32),
+            pltpu.VMEM((n_chunk, n_side, n_side, rows, block), f32),
+            pltpu.VMEM((n_chunk, n_side - 1, n_side, rows, block), f32),
+            pltpu.VMEM((n_chunk, n_side, rows, block), f32),
+            pltpu.VMEM((n_chunk, n_side - 1, rows, block), f32),
+            pltpu.VMEM((n_chunk, n_z, urows, block), f32),
+            pltpu.VMEM((n_chunk, n_z - 1, urows, block), f32),
+            dma((2,)),
+            dma((2,)),
+            dma((n_chunk, n_side - 1)),
+            dma((n_chunk, n_side - 1)),
+            dma((n_chunk, n_side - 1)),
+            dma((n_chunk, n_side - 1)),
+            dma((n_chunk, n_z - 1)),
+            dma((n_chunk, n_z - 1)),
+        ],
+        compiler_params=pltpu.CompilerParams(
+            collective_id=0, has_side_effects=True, vmem_limit_bytes=56 << 20
+        ),
+    )(image, window_rows.reshape(1, -1), window_cols.reshape(1, -1), *scalars)
+
+
 def solution(mesh):
+    n_side = mesh.shape["fcol"] // 2
+    n_z = mesh.shape["frow"] // n_side
+    tiled = (
+        n_side >= 2
+        and n_z >= 2
+        and mesh.shape["fcol"] == 2 * n_side
+        and mesh.shape["frow"] == n_z * n_side
+        and SG % (2 * n_side * 128) == 0
+        and SG % (n_side * n_z * ROWS) == 0
+    )
+
+    def local(image, *rest):
+        if tiled and image.shape[1] == image.shape[2] and image.shape[1] % 128 == 0:
+            return fused_local(n_side, n_z, image, *rest)
+        return general_local(image, *rest)
+
     placed = (P(None, "frow", "fcol"), P("frow"), P("fcol"), P(), P(), P(), P(), P(), P())
     return jax.shard_map(
         local, mesh=mesh, in_specs=placed, out_specs=P(None, None, "frow", "fcol"), check_vma=False

time: 174 us -> 42.7 us (0.25)
  waiting for transfers between devices: 89.3 us -> 0 us
  other arithmetic: 59.1 us -> 0 us
  Pallas kernels: 0 us -> 41 us
  between operations: 13.6 us -> 0.01 us
  matrix products: 6.43 us -> 0 us
  local copies, waits for them, and re-layouts: 4.76 us -> 1.57 us
    reduce_scatter x2 -> x0, waiting for transfers between devices: 89.3 us -> none  [the longest x1 64.7 us: local(): return lax.psum_scatter(term, 'frow', scatter_dimension=2, tiled=True)]
    pallas_call x0 -> x1, Pallas kernels: none -> 41 us  [fused_local(): pl.pallas_call(functools.partial(fused_kernel, (n_side, n_z, n_sub, facet...]
    convert_element_type x4 -> x0, other arithmetic: 30.9 us -> none  [the longest x2 19.9 us: dft_table(): (-jnp.sin(angle)).astype(jnp.bfloat16)]
    neg x2 -> x0, other arithmetic: 19.7 us -> none  [the longest x1 10.2 us: block_table(): lower = jnp.concatenate([-table_im, table_re], axis=1)]
    dot_general x3 -> x0, matrix products: 6.43 us -> none  [the longest x1 3.83 us: local(): jnp.einsum('kxcu,kxv->kcuv', left_side, right_side, preferred_element_typ...]
    another operation x2 -> x0, other arithmetic: 4.4 us -> none  [the longest x1 2.39 us: local(): jnp.stack(outputs, axis=1)]
    dynamic_slice x2 -> x0, local copies, waits for them, and re-layouts: 1.98 us -> none  [the longest x1 1.4 us: local(): facet_col_offset[fcol_index] + jnp.arange(image.shape[2], dtype=jnp.int32)]
    slice x2 -> x0, local copies, waits for them, and re-layouts: 1.9 us -> none  [the longest x1 1.31 us: local(): band_offset[column] + freqs[None, :]]
  transfers between devices with their start and end apart: 2 -> 0, of which waited for: 2 -> 0; matrix products, arithmetic and copies ran while one was open for 13% -> 0% of each run, Pallas kernels for 0% -> 0%
where the time goes in v1:
time: 42.7 us; the launch traced here: 42.5 us
  Pallas kernels  41 us (96%)
  local copies, waits for them, and re-layouts  1.57 us (4%)
    pallas_call x1, Pallas kernels, fused_local(): pl.pallas_call(functools.partial(fused_kernel, (n_side, n_z, n_sub, facet...  41 us
    unnamed x1, local copies, waits for them, and re-layouts  1.57 us

profile of v1, /device:TPU:0, one launch (start us, length us, event | category | flops | bytes accessed | tf_op | source)
XLA Modules:
  0.0 42.5 jit_solution(11976827133320649986)
XLA Ops:
  0.0 41.0 %shard_map.91 = f32[2,2,64,128]{3,2,1,0:T(8,128)} custom-call(bf16[2,512,512]{2,1,0:T(8,128)(2,1)} %image_ref.1, f32[1,512]{1,0:T(1,128)} %bitcast.2, f32[1,512]{1,0:T(1,128)} %bitcast.3, f32[2]{0:T(128)} %w_ref.1, s32[8]{0:T(128)} %row_off_ref.1, s32[4]{0:T(128)} %col_off_ref.1, s32[2]{0:T(128)} %band_ref.1, s32[2]{0:T(128)} %sub_off_ref.1, s32[2]{0:T(128)} %sub_col_ref.1), custom_call_target="tpu_custom_call" | custom-call | tf_op jit(solution)/shard_map/pallas_call | solution.py:362
  41.0 1.6 %copy.11 = f32[2,2,64,128]{3,2,1,0:T(8,128)} copy(f32[2,2,64,128]{3,2,1,0:T(8,128)} %shard_map.91) | data formatting | bytes 262144

commit v2 on v1

--- a/solution.py
+++ b/solution.py
@@ -97,6 +97,7 @@
 
 MESH = pl.DeviceIdType.MESH
 ROWS = 16
+PARTS = 2
 
 
 def unit_phasor(index):
@@ -134,11 +135,11 @@
 
 def fused_kernel(
     dims,
-    image_ref, wrow_ref, wcol_ref, w_ref, row_off_ref, col_off_ref, band_ref, sub_off_ref, sub_col_ref,
+    image_hbm, wrow_ref, wcol_ref, w_ref, row_off_ref, col_off_ref, band_ref, sub_off_ref, sub_col_ref,
     out_ref,
-    send, got, wsend, wgot, left, right, band, rtab, coarse, fine, phases,
+    left, right, hown, hsend, hgot, band, rtab, coarse, fine, phases,
     part, recv1, sum1, recv2, sum2, recv3,
-    isend, irecv, s1, r1, s2, r2, s3, r3,
+    lsem, isend, irecv, s1, r1, s2, r2, s3, r3,
 ):
     n_side, n_z, n_sub, facet, sg = dims
     r = lax.axis_index("frow")
@@ -147,6 +148,7 @@
     z, y = r // n_side, r % n_side
     block = sg // (2 * n_side)
     urows = sg // (n_side * n_z)
+    up = urows // PARTS
     nv = sg // 2
     partner = (r, c + 1 - 2 * core)
     first = x * (1 - core) + y * core
@@ -161,20 +163,26 @@
     seconds = [(second + d) % n_side for d in range(1, n_side)]
     zs = [(z + d) % n_z for d in range(1, n_z)]
     peers = (
-        [partner]
+        [place(first, second, q) for q in zs]
         + [place(a, second, z) for a in firsts]
         + [place(first, b, z) for b in seconds]
-        + [place(first, second, q) for q in zs]
+        + [partner]
     )
     barrier = pltpu.get_barrier_semaphore()
     for peer in peers:
         pl.semaphore_signal(barrier, inc=1, device_id=peer, device_id_type=MESH)
 
-    send[...] = image_ref[...].astype(jnp.float32)
-    wsend[...] = jnp.broadcast_to(wcol_ref[...], wsend.shape)
+    loads = [
+        pltpu.make_async_copy(
+            image_hbm.at[i], left.at[:, i * facet : (i + 1) * facet], lsem.at[i]
+        )
+        for i in range(2)
+    ]
+    for load in loads:
+        load.start()
 
     lane = iota((1, facet), 1)
-    gcol = [col_off_ref[c] + lane, col_off_ref[partner[1]] + lane]
+    gcol = col_off_ref[c] + lane
     grow = row_off_ref[r] + lane
     columns = [sub_col_ref[k] for k in range(n_sub)]
 
@@ -182,8 +190,8 @@
     angle = jnp.zeros((phases.shape[1], facet), jnp.float32)
     for k in range(n_sub):
         w = w_ref[columns[k]]
-        for f, coords in enumerate(gcol + [grow]):
-            angle = jnp.where(row_id == 3 * k + f, w * coord_square(coords), angle)
+        for f, coords in enumerate((gcol, grow)):
+            angle = jnp.where(row_id == 2 * k + f, w * coord_square(coords), angle)
     phases[0] = jnp.cos(angle)
     phases[1] = jnp.sin(angle)
 
@@ -197,8 +205,8 @@
             unit_phasor(residue(coords, freqs)),
             (phases[0, row : row + 1, :] * gain, phases[1, row : row + 1, :] * gain),
         )
-        coarse[0, : freqs.shape[0]] = p[0]
-        coarse[1, : freqs.shape[0]] = p[1]
+        coarse[0] = p[0]
+        coarse[1] = p[1]
 
     def entries(h):
         re, im = times(
@@ -206,23 +214,22 @@
         )
         return re.astype(jnp.bfloat16), im.astype(jnp.bfloat16)
 
-    def build_columns(f):
-        write_fine(gcol[f])
-        gain = wcol_ref[...] if f == 0 else wgot[0:1, :]
-        at = 2 * facet * f
-        for k in range(n_sub):
-            index = iota((nv // ROWS, facet), 0) * ROWS
-            v = block * (2 * (index // block) + core) + index % block
-            write_coarse(gcol[f], band_ref[columns[k]] + v, gain, 3 * k + f)
-
-            def body(h, carry, k=k):
-                re, im = entries(h)
+    def build_columns(k):
+        index = iota((sg // ROWS, facet), 0) * ROWS
+        owner = (core + index // nv) % 2
+        inner = index % nv
+        v = block * (2 * (inner // block) + owner) + inner % block
+        write_coarse(gcol, band_ref[columns[k]] + v, wcol_ref[...], 2 * k)
+        for side in range(2):
+
+            def body(h, carry, side=side):
+                re, im = entries(side * (nv // ROWS) + h)
                 top = pl.ds(pl.multiple_of(h * ROWS, ROWS), ROWS)
                 low = pl.ds(pl.multiple_of(nv + h * ROWS, ROWS), ROWS)
-                right[k, top, at : at + facet] = re
-                right[k, top, at + facet : at + 2 * facet] = -im
-                right[k, low, at : at + facet] = im
-                right[k, low, at + facet : at + 2 * facet] = re
+                right[side, k, top, :facet] = re
+                right[side, k, top, facet:] = -im
+                right[side, k, low, :facet] = im
+                right[side, k, low, facet:] = re
                 return carry
 
             lax.fori_loop(0, nv // ROWS, body, 0)
@@ -231,10 +238,14 @@
         write_fine(grow)
         for k in range(n_sub):
             index = iota((sg // ROWS, facet), 0) * ROWS
-            per = sg // n_side
-            u = urows * (n_side * (index % per // urows) + index // per) + index % urows
-            gain = wrow_ref[...] * dims_scale
-            write_coarse(grow, sub_off_ref[k] + u, gain, 3 * k + 2)
+            inner = index % (sg // PARTS)
+            per = up * n_z
+            u = (
+                urows * (n_side * (inner % per // up) + inner // per)
+                + up * (index // (sg // PARTS))
+                + index % up
+            )
+            write_coarse(grow, sub_off_ref[k] + u, wrow_ref[...] * scale, 2 * k + 1)
 
             def body(h, carry, k=k):
                 re, im = entries(h)
@@ -247,63 +258,64 @@
 
             lax.fori_loop(0, sg // ROWS, body, 0)
 
-    dims_scale = 1.0 / math.sqrt(facet * lax.axis_size("fcol")) / math.sqrt(facet * lax.axis_size("frow"))
+    scale = 1.0 / math.sqrt(facet * lax.axis_size("fcol")) / math.sqrt(facet * lax.axis_size("frow"))
 
     def remote(src, dst, a, b, peer):
         return pltpu.make_async_remote_copy(
             src_ref=src, dst_ref=dst, send_sem=a, recv_sem=b, device_id=peer, device_id_type=MESH
         )
 
+    write_fine(gcol)
+    for k in range(n_sub):
+        build_columns(k)
+    for load in loads:
+        load.wait()
+    for k in range(n_sub):
+        for side, target in ((1, hsend), (0, hown)):
+            target[k] = lax.dot_general(
+                left[...],
+                right[side, k],
+                (((1,), (1,)), ((), ())),
+                preferred_element_type=jnp.float32,
+            )
     pl.semaphore_wait(barrier, len(peers))
-    wcopy = remote(wsend, wgot, isend.at[0], irecv.at[0], partner)
-    icopy = remote(send, got, isend.at[1], irecv.at[1], partner)
-    wcopy.start()
-    icopy.start()
-    left[:, :facet] = image_ref[0]
-    left[:, facet : 2 * facet] = image_ref[1]
-    build_columns(0)
-    wcopy.wait()
-    build_columns(1)
+    swaps = [
+        remote(hsend.at[k], hgot.at[k], isend.at[k], irecv.at[k], partner) for k in range(n_sub)
+    ]
+    for swap in swaps:
+        swap.start()
     build_rows()
-    icopy.wait()
-    left[:, 2 * facet : 3 * facet] = got[0].astype(jnp.bfloat16)
-    left[:, 3 * facet :] = got[1].astype(jnp.bfloat16)
-
-    n_chunk = 2 * n_sub
+
+    n_chunk = 2 * n_sub * PARTS
+    where = [(k, half, p) for k in range(n_sub) for half in range(2) for p in range(PARTS)]
     copies1, copies2, copies3 = [], [], []
-    step = 128
-    for k in range(n_sub):
-
-        def contract(i, carry, k=k):
-            at = pl.ds(pl.multiple_of(i * step, step), step)
-            value = lax.dot_general(
-                left[at, :], right[k], (((1,), (1,)), ((), ())), preferred_element_type=jnp.float32
-            ).astype(jnp.bfloat16)
-            band[k, at, :] = value[:, :nv]
-            band[k, pl.ds(pl.multiple_of(facet + i * step, step), step), :] = value[:, nv:]
-            return carry
-
-        lax.fori_loop(0, facet // step, contract, 0)
-        for half in range(2):
-            ch = 2 * k + half
-            rows = sg // n_side
-            for yb in range(n_side):
-                value = jnp.dot(
-                    rtab[k, half, yb * rows : (yb + 1) * rows, :],
-                    band[k],
-                    preferred_element_type=jnp.float32,
+    rows = up * n_z
+    for ch, (k, half, p) in enumerate(where):
+        if half == 0 and p == 0:
+            swaps[k].wait_recv()
+            for i in range(2):
+                at = slice(i * nv, (i + 1) * nv)
+                band[k, i * facet : (i + 1) * facet, :] = (hown[k, :, at] + hgot[k, :, at]).astype(
+                    jnp.bfloat16
                 )
-                for xb in range(n_side):
-                    a = xb * (1 - core) + yb * core
-                    b = yb * (1 - core) + xb * core
-                    part[ch, a, b] = value[:, xb * block : (xb + 1) * block]
-            group = [
-                remote(part.at[ch, a], recv1.at[ch, d], s1.at[ch, d], r1.at[ch, d], place(a, second, z))
-                for d, a in enumerate(firsts)
-            ]
-            for copy in group:
-                copy.start()
-            copies1.append(group)
+        span = sg // PARTS
+        value = jnp.dot(
+            rtab[k, half, p * span : (p + 1) * span, :],
+            band[k],
+            preferred_element_type=jnp.float32,
+        )
+        for yb in range(n_side):
+            for xb in range(n_side):
+                a = xb * (1 - core) + yb * core
+                b = yb * (1 - core) + xb * core
+                part[ch, a, b] = value[yb * rows : (yb + 1) * rows, xb * block : (xb + 1) * block]
+        group = [
+            remote(part.at[ch, a], recv1.at[ch, d], s1.at[ch, d], r1.at[ch, d], place(a, second, z))
+            for d, a in enumerate(firsts)
+        ]
+        for copy in group:
+            copy.start()
+        copies1.append(group)
 
     for t in range(n_chunk + 1):
         if t < n_chunk:
@@ -328,7 +340,7 @@
             total = sum1[ch, second]
             for d in range(n_side - 1):
                 total = total + recv2[ch, d]
-            sum2[ch] = total.reshape(n_z, urows, block)
+            sum2[ch] = total.reshape(n_z, up, block)
             group = [
                 remote(sum2.at[ch, q], recv3.at[ch, d], s3.at[ch, d], r3.at[ch, d], place(first, second, q))
                 for d, q in enumerate(zs)
@@ -336,13 +348,15 @@
             for copy in group:
                 copy.start()
             copies3.append(group)
-    for ch in range(n_chunk):
+    for ch, (k, half, p) in enumerate(where):
         for copy in copies3[ch]:
             copy.wait_recv()
         total = sum2[ch, z]
         for d in range(n_z - 1):
             total = total + recv3[ch, d]
-        out_ref[ch // 2, ch % 2] = total
+        out_ref[k, half, p * up : (p + 1) * up, :] = total
+    for swap in swaps:
+        swap.wait_send()
     for group in copies1 + copies2 + copies3:
         for copy in group:
             copy.wait_send()
@@ -351,10 +365,11 @@
 def fused_local(n_side, n_z, image, window_rows, window_cols, *scalars):
     facet = image.shape[1]
     n_sub = scalars[4].shape[0]
-    n_chunk = 2 * n_sub
+    n_chunk = 2 * n_sub * PARTS
     block = SG // (2 * n_side)
     urows = SG // (n_side * n_z)
-    rows = SG // n_side
+    up = urows // PARTS
+    rows = up * n_z
     f32, b16 = jnp.float32, jnp.bfloat16
     vmem = pl.BlockSpec(memory_space=pltpu.VMEM)
     smem = pl.BlockSpec(memory_space=pltpu.SMEM)
@@ -362,28 +377,28 @@
     return pl.pallas_call(
         functools.partial(fused_kernel, (n_side, n_z, n_sub, facet, SG)),
         out_shape=jax.ShapeDtypeStruct((n_sub, 2, urows, block), f32),
-        in_specs=[vmem] * 3 + [smem] * 6,
+        in_specs=[pl.BlockSpec(memory_space=pl.ANY)] + [vmem] * 2 + [smem] * 6,
         out_specs=vmem,
         scratch_shapes=[
-            pltpu.VMEM(image.shape, f32),
-            pltpu.VMEM(image.shape, f32),
-            pltpu.VMEM((8, facet), f32),
-            pltpu.VMEM((8, facet), f32),
-            pltpu.VMEM((facet, 4 * facet), b16),
-            pltpu.VMEM((n_sub, SG, 4 * facet), b16),
+            pltpu.VMEM((facet, 2 * facet), b16),
+            pltpu.VMEM((2, n_sub, SG, 2 * facet), b16),
+            pltpu.VMEM((n_sub, facet, SG), f32),
+            pltpu.VMEM((n_sub, facet, SG), f32),
+            pltpu.VMEM((n_sub, facet, SG), f32),
             pltpu.VMEM((n_sub, 2 * facet, SG // 2), b16),
             pltpu.VMEM((n_sub, 2, SG, 2 * facet), b16),
             pltpu.VMEM((2, SG // ROWS, facet), f32),
             pltpu.VMEM((2, ROWS, facet), f32),
-            pltpu.VMEM((2, -(-3 * n_sub // 8) * 8, facet), f32),
+            pltpu.VMEM((2, -(-2 * n_sub // 8) * 8, facet), f32),
             pltpu.VMEM((n_chunk, n_side, n_side, rows, block), f32),
             pltpu.VMEM((n_chunk, n_side - 1, n_side, rows, block), f32),
             pltpu.VMEM((n_chunk, n_side, rows, block), f32),
             pltpu.VMEM((n_chunk, n_side - 1, rows, block), f32),
-            pltpu.VMEM((n_chunk, n_z, urows, block), f32),
-            pltpu.VMEM((n_chunk, n_z - 1, urows, block), f32),
+            pltpu.VMEM((n_chunk, n_z, up, block), f32),
+            pltpu.VMEM((n_chunk, n_z - 1, up, block), f32),
             dma((2,)),
-            dma((2,)),
+            dma((n_sub,)),
+            dma((n_sub,)),
             dma((n_chunk, n_side - 1)),
             dma((n_chunk, n_side - 1)),
             dma((n_chunk, n_side - 1)),
@@ -406,7 +421,7 @@
         and mesh.shape["fcol"] == 2 * n_side
         and mesh.shape["frow"] == n_z * n_side
         and SG % (2 * n_side * 128) == 0
-        and SG % (n_side * n_z * ROWS) == 0
+        and SG % (n_side * n_z * ROWS * PARTS) == 0
     )
 
     def local(image, *rest):

time: 42.7 us -> 40.1 us (0.939)
  Pallas kernels: 41 us -> 38.4 us
    pallas_call x1, Pallas kernels: 41 us -> 38.4 us  [fused_local(): pl.pallas_call(functools.partial(fused_kernel, (n_side, n_z, n_sub, facet...]
where the time goes in v2:
time: 40.1 us; the launch traced here: 40 us
  Pallas kernels  38.4 us (96%)
  local copies, waits for them, and re-layouts  1.57 us (4%)
    pallas_call x1, Pallas kernels, fused_local(): pl.pallas_call(functools.partial(fused_kernel, (n_side, n_z, n_sub, facet...  38.4 us
    unnamed x1, local copies, waits for them, and re-layouts  1.57 us

profile of v2, /device:TPU:0, one launch (start us, length us, event | category | flops | bytes accessed | tf_op | source)
XLA Modules:
  0.0 40.0 jit_solution(4195023396730297918)
XLA Ops:
  0.0 38.4 %shard_map.91 = f32[2,2,64,128]{3,2,1,0:T(8,128)} custom-call(bf16[2,512,512]{2,1,0:T(8,128)(2,1)} %image_hbm.1, f32[1,512]{1,0:T(1,128)} %bitcast.2, f32[1,512]{1,0:T(1,128)} %bitcast.3, f32[2]{0:T(128)} %w_ref.1, s32[8]{0:T(128)} %row_off_ref.1, s32[4]{0:T(128)} %col_off_ref.1, s32[2]{0:T(128)} %band_ref.1, s32[2]{0:T(128)} %sub_off_ref.1, s32[2]{0:T(128)} %sub_col_ref.1), custom_call_target="tpu_custom_call" | custom-call | tf_op jit(solution)/shard_map/pallas_call | solution.py:377
  38.4 1.6 %copy.11 = f32[2,2,64,128]{3,2,1,0:T(8,128)} copy(f32[2,2,64,128]{3,2,1,0:T(8,128)} %shard_map.91) | data formatting | bytes 262144

commit v3 on v2

--- a/solution.py
+++ b/solution.py
@@ -138,8 +138,8 @@
     image_hbm, wrow_ref, wcol_ref, w_ref, row_off_ref, col_off_ref, band_ref, sub_off_ref, sub_col_ref,
     out_ref,
     left, right, hown, hsend, hgot, band, rtab, coarse, fine, phases,
-    part, recv1, sum1, recv2, sum2, recv3,
-    lsem, isend, irecv, s1, r1, s2, r2, s3, r3,
+    part, recv1, sum1, recv2, sum2, recv3, zpart, zrecv1, zsum1, zrecv2, zsum2, zrecv3,
+    lsem, isend, irecv, s1, r1, s2, r2, s3, r3, t1, q1, t2, q2, t3, q3,
 ):
     n_side, n_z, n_sub, facet, sg = dims
     r = lax.axis_index("frow")
@@ -268,6 +268,7 @@
     write_fine(gcol)
     for k in range(n_sub):
         build_columns(k)
+    build_rows()
     for load in loads:
         load.wait()
     for k in range(n_sub):
@@ -284,8 +285,6 @@
     ]
     for swap in swaps:
         swap.start()
-    build_rows()
-
     n_chunk = 2 * n_sub * PARTS
     where = [(k, half, p) for k in range(n_sub) for half in range(2) for p in range(PARTS)]
     copies1, copies2, copies3 = [], [], []
@@ -308,7 +307,22 @@
             for xb in range(n_side):
                 a = xb * (1 - core) + yb * core
                 b = yb * (1 - core) + xb * core
-                part[ch, a, b] = value[yb * rows : (yb + 1) * rows, xb * block : (xb + 1) * block]
+                tile = value[yb * rows : (yb + 1) * rows, xb * block : (xb + 1) * block]
+                if ch == 0:
+                    for zz in range(n_z):
+                        zpart[zz, a, b] = tile[zz * up : (zz + 1) * up]
+                else:
+                    part[ch, a, b] = tile
+        if ch == 0:
+            zcopies = [
+                [
+                    remote(zpart.at[q], zrecv1.at[d], t1.at[d], q1.at[d], place(first, second, q))
+                    for d, q in enumerate(zs)
+                ]
+            ]
+            for copy in zcopies[0]:
+                copy.start()
+            continue
         group = [
             remote(part.at[ch, a], recv1.at[ch, d], s1.at[ch, d], r1.at[ch, d], place(a, second, z))
             for d, a in enumerate(firsts)
@@ -317,47 +331,69 @@
             copy.start()
         copies1.append(group)
 
-    for t in range(n_chunk + 1):
-        if t < n_chunk:
-            ch = t
-            for copy in copies1[ch]:
-                copy.wait_recv()
-            total = part[ch, first]
-            for d in range(n_side - 1):
-                total = total + recv1[ch, d]
-            sum1[ch] = total
-            group = [
-                remote(sum1.at[ch, b], recv2.at[ch, d], s2.at[ch, d], r2.at[ch, d], place(first, b, z))
+    def advance(group, own, arrived):
+        for copy in group:
+            copy.wait_recv()
+        total = own
+        for d in range(len(group)):
+            total = total + arrived[d]
+        return total
+
+    def launch(group):
+        for copy in group:
+            copy.start()
+        return group
+
+    for ch in range(1, n_chunk + 1):
+        if ch < n_chunk:
+            sum1[ch] = advance(copies1[ch - 1], part[ch, first], recv1.at[ch])
+            copies2.append(
+                launch(
+                    [
+                        remote(sum1.at[ch, b], recv2.at[ch, d], s2.at[ch, d], r2.at[ch, d], place(first, b, z))
+                        for d, b in enumerate(seconds)
+                    ]
+                )
+            )
+        if ch == n_chunk // 2:
+            zsum1[...] = advance(zcopies[0], zpart[z], zrecv1)
+            zcopies.append(
+                launch(
+                    [
+                        remote(zsum1.at[a], zrecv2.at[d], t2.at[d], q2.at[d], place(a, second, z))
+                        for d, a in enumerate(firsts)
+                    ]
+                )
+            )
+        if ch >= 2:
+            done = ch - 1
+            total = advance(copies2[done - 1], sum1[done, second], recv2.at[done])
+            sum2[done] = total.reshape(n_z, up, block)
+            copies3.append(
+                launch(
+                    [
+                        remote(sum2.at[done, q], recv3.at[done, d], s3.at[done, d], r3.at[done, d], place(first, second, q))
+                        for d, q in enumerate(zs)
+                    ]
+                )
+            )
+    zsum2[...] = advance(zcopies[1], zsum1[first], zrecv2)
+    zcopies.append(
+        launch(
+            [
+                remote(zsum2.at[b], zrecv3.at[d], t3.at[d], q3.at[d], place(first, b, z))
                 for d, b in enumerate(seconds)
             ]
-            for copy in group:
-                copy.start()
-            copies2.append(group)
-        if t >= 1:
-            ch = t - 1
-            for copy in copies2[ch]:
-                copy.wait_recv()
-            total = sum1[ch, second]
-            for d in range(n_side - 1):
-                total = total + recv2[ch, d]
-            sum2[ch] = total.reshape(n_z, up, block)
-            group = [
-                remote(sum2.at[ch, q], recv3.at[ch, d], s3.at[ch, d], r3.at[ch, d], place(first, second, q))
-                for d, q in enumerate(zs)
-            ]
-            for copy in group:
-                copy.start()
-            copies3.append(group)
+        )
+    )
     for ch, (k, half, p) in enumerate(where):
-        for copy in copies3[ch]:
-            copy.wait_recv()
-        total = sum2[ch, z]
-        for d in range(n_z - 1):
-            total = total + recv3[ch, d]
-        out_ref[k, half, p * up : (p + 1) * up, :] = total
+        if ch > 0:
+            total = advance(copies3[ch - 1], sum2[ch, z], recv3.at[ch])
+            out_ref[k, half, p * up : (p + 1) * up, :] = total
+    out_ref[0, 0, :up, :] = advance(zcopies[2], zsum2[second], zrecv3)
     for swap in swaps:
         swap.wait_send()
-    for group in copies1 + copies2 + copies3:
+    for group in copies1 + copies2 + copies3 + zcopies:
         for copy in group:
             copy.wait_send()
 
@@ -396,6 +432,12 @@
             pltpu.VMEM((n_chunk, n_side - 1, rows, block), f32),
             pltpu.VMEM((n_chunk, n_z, up, block), f32),
             pltpu.VMEM((n_chunk, n_z - 1, up, block), f32),
+            pltpu.VMEM((n_z, n_side, n_side, up, block), f32),
+            pltpu.VMEM((n_z - 1, n_side, n_side, up, block), f32),
+            pltpu.VMEM((n_side, n_side, up, block), f32),
+            pltpu.VMEM((n_side - 1, n_side, up, block), f32),
+            pltpu.VMEM((n_side, up, block), f32),
+            pltpu.VMEM((n_side - 1, up, block), f32),
             dma((2,)),
             dma((n_sub,)),
             dma((n_sub,)),
@@ -405,6 +447,12 @@
             dma((n_chunk, n_side - 1)),
             dma((n_chunk, n_z - 1)),
             dma((n_chunk, n_z - 1)),
+            dma((n_z - 1,)),
+            dma((n_z - 1,)),
+            dma((n_side - 1,)),
+            dma((n_side - 1,)),
+            dma((n_side - 1,)),
+            dma((n_side - 1,)),
         ],
         compiler_params=pltpu.CompilerParams(
             collective_id=0, has_side_effects=True, vmem_limit_bytes=56 << 20

time: 40.1 us -> 39.7 us (0.990)
  Pallas kernels: 38.4 us -> 37.9 us
    pallas_call x1, Pallas kernels: 38.4 us -> 37.9 us  [fused_local(): pl.pallas_call(functools.partial(fused_kernel, (n_side, n_z, n_sub, facet...]
where the time goes in v3:
time: 39.7 us; the launch traced here: 39.5 us
  Pallas kernels  37.9 us (95%)
  local copies, waits for them, and re-layouts  1.57 us (4%)
    pallas_call x1, Pallas kernels, fused_local(): pl.pallas_call(functools.partial(fused_kernel, (n_side, n_z, n_sub, facet...  37.9 us
    unnamed x1, local copies, waits for them, and re-layouts  1.57 us

profile of v3, /device:TPU:0, one launch (start us, length us, event | category | flops | bytes accessed | tf_op | source)
XLA Modules:
  0.0 39.5 jit_solution(10425020567606784112)
XLA Ops:
  0.0 37.9 %shard_map.91 = f32[2,2,64,128]{3,2,1,0:T(8,128)} custom-call(bf16[2,512,512]{2,1,0:T(8,128)(2,1)} %image_hbm.1, f32[1,512]{1,0:T(1,128)} %bitcast.2, f32[1,512]{1,0:T(1,128)} %bitcast.3, f32[2]{0:T(128)} %w_ref.1, s32[8]{0:T(128)} %row_off_ref.1, s32[4]{0:T(128)} %col_off_ref.1, s32[2]{0:T(128)} %band_ref.1, s32[2]{0:T(128)} %sub_off_ref.1, s32[2]{0:T(128)} %sub_col_ref.1), custom_call_target="tpu_custom_call" | custom-call | tf_op jit(solution)/shard_map/pallas_call | solution.py:413
  37.9 1.6 %copy.11 = f32[2,2,64,128]{3,2,1,0:T(8,128)} copy(f32[2,2,64,128]{3,2,1,0:T(8,128)} %shard_map.91) | data formatting | bytes 262144

commit v4 on v3

--- a/solution.py
+++ b/solution.py
@@ -195,10 +195,10 @@
     phases[0] = jnp.cos(angle)
     phases[1] = jnp.sin(angle)
 
-    def write_fine(coords):
+    def write_fine(slot, coords):
         q = unit_phasor(residue(coords, iota((ROWS, facet), 0)))
-        fine[0] = q[0]
-        fine[1] = q[1]
+        fine[slot, 0] = q[0]
+        fine[slot, 1] = q[1]
 
     def write_coarse(coords, freqs, gain, row):
         p = times(
@@ -208,9 +208,9 @@
         coarse[0] = p[0]
         coarse[1] = p[1]
 
-    def entries(h):
+    def entries(slot, h):
         re, im = times(
-            (coarse[0, pl.ds(h, 1), :], coarse[1, pl.ds(h, 1), :]), (fine[0], fine[1])
+            (coarse[0, pl.ds(h, 1), :], coarse[1, pl.ds(h, 1), :]), (fine[slot, 0], fine[slot, 1])
         )
         return re.astype(jnp.bfloat16), im.astype(jnp.bfloat16)
 
@@ -223,7 +223,7 @@
         for side in range(2):
 
             def body(h, carry, side=side):
-                re, im = entries(side * (nv // ROWS) + h)
+                re, im = entries(0, side * (nv // ROWS) + h)
                 top = pl.ds(pl.multiple_of(h * ROWS, ROWS), ROWS)
                 low = pl.ds(pl.multiple_of(nv + h * ROWS, ROWS), ROWS)
                 right[side, k, top, :facet] = re
@@ -234,29 +234,27 @@
 
             lax.fori_loop(0, nv // ROWS, body, 0)
 
-    def build_rows():
-        write_fine(grow)
-        for k in range(n_sub):
-            index = iota((sg // ROWS, facet), 0) * ROWS
-            inner = index % (sg // PARTS)
-            per = up * n_z
-            u = (
-                urows * (n_side * (inner % per // up) + inner // per)
-                + up * (index // (sg // PARTS))
-                + index % up
-            )
-            write_coarse(grow, sub_off_ref[k] + u, wrow_ref[...] * scale, 2 * k + 1)
-
-            def body(h, carry, k=k):
-                re, im = entries(h)
-                at = pl.ds(pl.multiple_of(h * ROWS, ROWS), ROWS)
-                rtab[k, 0, at, :facet] = re
-                rtab[k, 0, at, facet:] = -im
-                rtab[k, 1, at, :facet] = im
-                rtab[k, 1, at, facet:] = re
-                return carry
-
-            lax.fori_loop(0, sg // ROWS, body, 0)
+    def build_rows(k):
+        index = iota((sg // ROWS, facet), 0) * ROWS
+        inner = index % (sg // PARTS)
+        per = up * n_z
+        u = (
+            urows * (n_side * (inner % per // up) + inner // per)
+            + up * (index // (sg // PARTS))
+            + index % up
+        )
+        write_coarse(grow, sub_off_ref[k] + u, wrow_ref[...] * scale, 2 * k + 1)
+
+        def body(h, carry):
+            re, im = entries(1, h)
+            at = pl.ds(pl.multiple_of(h * ROWS, ROWS), ROWS)
+            rtab[k, 0, at, :facet] = re
+            rtab[k, 0, at, facet:] = -im
+            rtab[k, 1, at, :facet] = im
+            rtab[k, 1, at, facet:] = re
+            return carry
+
+        lax.fori_loop(0, sg // ROWS, body, 0)
 
     scale = 1.0 / math.sqrt(facet * lax.axis_size("fcol")) / math.sqrt(facet * lax.axis_size("frow"))
 
@@ -265,39 +263,32 @@
             src_ref=src, dst_ref=dst, send_sem=a, recv_sem=b, device_id=peer, device_id_type=MESH
         )
 
-    write_fine(gcol)
-    for k in range(n_sub):
-        build_columns(k)
-    build_rows()
-    for load in loads:
-        load.wait()
-    for k in range(n_sub):
-        for side, target in ((1, hsend), (0, hown)):
-            target[k] = lax.dot_general(
-                left[...],
-                right[side, k],
-                (((1,), (1,)), ((), ())),
-                preferred_element_type=jnp.float32,
-            )
-    pl.semaphore_wait(barrier, len(peers))
-    swaps = [
-        remote(hsend.at[k], hgot.at[k], isend.at[k], irecv.at[k], partner) for k in range(n_sub)
-    ]
-    for swap in swaps:
-        swap.start()
+    def contract(side, k):
+        return lax.dot_general(
+            left[...], right[side, k], (((1,), (1,)), ((), ())), preferred_element_type=jnp.float32
+        )
+
+    def advance(group, own, arrived):
+        for copy in group:
+            copy.wait_recv()
+        total = own
+        for d in range(len(group)):
+            total = total + arrived[d]
+        return total
+
+    def launch(group):
+        for copy in group:
+            copy.start()
+        return group
+
     n_chunk = 2 * n_sub * PARTS
     where = [(k, half, p) for k in range(n_sub) for half in range(2) for p in range(PARTS)]
-    copies1, copies2, copies3 = [], [], []
     rows = up * n_z
-    for ch, (k, half, p) in enumerate(where):
-        if half == 0 and p == 0:
-            swaps[k].wait_recv()
-            for i in range(2):
-                at = slice(i * nv, (i + 1) * nv)
-                band[k, i * facet : (i + 1) * facet, :] = (hown[k, :, at] + hgot[k, :, at]).astype(
-                    jnp.bfloat16
-                )
-        span = sg // PARTS
+    span = sg // PARTS
+    swaps, copies1, copies2, copies3, zcopies = [], [], [], [], []
+
+    def emit(ch):
+        k, half, p = where[ch]
         value = jnp.dot(
             rtab[k, half, p * span : (p + 1) * span, :],
             band[k],
@@ -314,69 +305,77 @@
                 else:
                     part[ch, a, b] = tile
         if ch == 0:
-            zcopies = [
-                [
-                    remote(zpart.at[q], zrecv1.at[d], t1.at[d], q1.at[d], place(first, second, q))
-                    for d, q in enumerate(zs)
-                ]
+            group = [
+                remote(zpart.at[q], zrecv1.at[d], t1.at[d], q1.at[d], place(first, second, q))
+                for d, q in enumerate(zs)
             ]
-            for copy in zcopies[0]:
-                copy.start()
-            continue
+            zcopies.append(launch(group))
+        else:
+            group = [
+                remote(part.at[ch, a], recv1.at[ch, d], s1.at[ch, d], r1.at[ch, d], place(a, second, z))
+                for d, a in enumerate(firsts)
+            ]
+            copies1.append(launch(group))
+
+    def finish_second():
+        done = len(copies3) + 1
+        total = advance(copies2[done - 1], sum1[done, second], recv2.at[done])
+        sum2[done] = total.reshape(n_z, up, block)
         group = [
-            remote(part.at[ch, a], recv1.at[ch, d], s1.at[ch, d], r1.at[ch, d], place(a, second, z))
-            for d, a in enumerate(firsts)
+            remote(sum2.at[done, q], recv3.at[done, d], s3.at[done, d], r3.at[done, d], place(first, second, q))
+            for d, q in enumerate(zs)
         ]
-        for copy in group:
-            copy.start()
-        copies1.append(group)
-
-    def advance(group, own, arrived):
-        for copy in group:
-            copy.wait_recv()
-        total = own
-        for d in range(len(group)):
-            total = total + arrived[d]
-        return total
-
-    def launch(group):
-        for copy in group:
-            copy.start()
-        return group
-
-    for ch in range(1, n_chunk + 1):
-        if ch < n_chunk:
-            sum1[ch] = advance(copies1[ch - 1], part[ch, first], recv1.at[ch])
-            copies2.append(
-                launch(
-                    [
-                        remote(sum1.at[ch, b], recv2.at[ch, d], s2.at[ch, d], r2.at[ch, d], place(first, b, z))
-                        for d, b in enumerate(seconds)
-                    ]
-                )
-            )
+        copies3.append(launch(group))
+
+    def pump():
+        ch = len(copies2) + 1
+        sum1[ch] = advance(copies1[ch - 1], part[ch, first], recv1.at[ch])
+        group = [
+            remote(sum1.at[ch, b], recv2.at[ch, d], s2.at[ch, d], r2.at[ch, d], place(first, b, z))
+            for d, b in enumerate(seconds)
+        ]
+        copies2.append(launch(group))
         if ch == n_chunk // 2:
             zsum1[...] = advance(zcopies[0], zpart[z], zrecv1)
-            zcopies.append(
-                launch(
-                    [
-                        remote(zsum1.at[a], zrecv2.at[d], t2.at[d], q2.at[d], place(a, second, z))
-                        for d, a in enumerate(firsts)
-                    ]
-                )
+            group = [
+                remote(zsum1.at[a], zrecv2.at[d], t2.at[d], q2.at[d], place(a, second, z))
+                for d, a in enumerate(firsts)
+            ]
+            zcopies.append(launch(group))
+        if ch >= 2:
+            finish_second()
+
+    write_fine(0, gcol)
+    for k in range(n_sub):
+        build_columns(k)
+        if k == 0:
+            for load in loads:
+                load.wait()
+        hsend[k] = contract(1, k)
+        if k == 0:
+            pl.semaphore_wait(barrier, len(peers))
+        swap = remote(hsend.at[k], hgot.at[k], isend.at[k], irecv.at[k], partner)
+        swap.start()
+        swaps.append(swap)
+        hown[k] = contract(0, k)
+        if k == 0:
+            write_fine(1, grow)
+        else:
+            pump()
+        build_rows(k)
+        swap.wait_recv()
+        for i in range(2):
+            at = slice(i * nv, (i + 1) * nv)
+            band[k, i * facet : (i + 1) * facet, :] = (hown[k, :, at] + hgot[k, :, at]).astype(
+                jnp.bfloat16
             )
-        if ch >= 2:
-            done = ch - 1
-            total = advance(copies2[done - 1], sum1[done, second], recv2.at[done])
-            sum2[done] = total.reshape(n_z, up, block)
-            copies3.append(
-                launch(
-                    [
-                        remote(sum2.at[done, q], recv3.at[done, d], s3.at[done, d], r3.at[done, d], place(first, second, q))
-                        for d, q in enumerate(zs)
-                    ]
-                )
-            )
+        for ch in range(2 * PARTS * k, 2 * PARTS * (k + 1)):
+            emit(ch)
+            if k > 0 and ch == 2 * PARTS * k + 1:
+                pump()
+    while len(copies2) < n_chunk - 1:
+        pump()
+    finish_second()
     zsum2[...] = advance(zcopies[1], zsum1[first], zrecv2)
     zcopies.append(
         launch(
@@ -424,7 +423,7 @@
             pltpu.VMEM((n_sub, 2 * facet, SG // 2), b16),
             pltpu.VMEM((n_sub, 2, SG, 2 * facet), b16),
             pltpu.VMEM((2, SG // ROWS, facet), f32),
-            pltpu.VMEM((2, ROWS, facet), f32),
+            pltpu.VMEM((2, 2, ROWS, facet), f32),
             pltpu.VMEM((2, -(-2 * n_sub // 8) * 8, facet), f32),
             pltpu.VMEM((n_chunk, n_side, n_side, rows, block), f32),
             pltpu.VMEM((n_chunk, n_side - 1, n_side, rows, block), f32),

time: 39.7 us -> 36.8 us (0.927)
  Pallas kernels: 37.9 us -> 35.1 us
    pallas_call x1, Pallas kernels: 37.9 us -> 35.1 us  [fused_local(): pl.pallas_call(functools.partial(fused_kernel, (n_side, n_z, n_sub, facet...]
where the time goes in v4:
time: 36.8 us; the launch traced here: 36.7 us
  Pallas kernels  35.1 us (95%)
  local copies, waits for them, and re-layouts  1.57 us (4%)
    pallas_call x1, Pallas kernels, fused_local(): pl.pallas_call(functools.partial(fused_kernel, (n_side, n_z, n_sub, facet...  35.1 us
    unnamed x1, local copies, waits for them, and re-layouts  1.57 us

profile of v4, /device:TPU:0, one launch (start us, length us, event | category | flops | bytes accessed | tf_op | source)
XLA Modules:
  0.0 36.7 jit_solution(11886715554231370727)
XLA Ops:
  0.0 35.1 %shard_map.91 = f32[2,2,64,128]{3,2,1,0:T(8,128)} custom-call(bf16[2,512,512]{2,1,0:T(8,128)(2,1)} %image_hbm.1, f32[1,512]{1,0:T(1,128)} %bitcast.2, f32[1,512]{1,0:T(1,128)} %bitcast.3, f32[2]{0:T(128)} %w_ref.1, s32[8]{0:T(128)} %row_off_ref.1, s32[4]{0:T(128)} %col_off_ref.1, s32[2]{0:T(128)} %band_ref.1, s32[2]{0:T(128)} %sub_off_ref.1, s32[2]{0:T(128)} %sub_col_ref.1), custom_call_target="tpu_custom_call" | custom-call | tf_op jit(solution)/shard_map/pallas_call | solution.py:412
  35.1 1.6 %copy.11 = f32[2,2,64,128]{3,2,1,0:T(8,128)} copy(f32[2,2,64,128]{3,2,1,0:T(8,128)} %shard_map.91) | data formatting | bytes 262144

commit v5 on v4

--- a/solution.py
+++ b/solution.py
@@ -214,25 +214,25 @@
         )
         return re.astype(jnp.bfloat16), im.astype(jnp.bfloat16)
 
-    def build_columns(k):
+    def column_phases(k):
         index = iota((sg // ROWS, facet), 0) * ROWS
         owner = (core + index // nv) % 2
         inner = index % nv
         v = block * (2 * (inner // block) + owner) + inner % block
         write_coarse(gcol, band_ref[columns[k]] + v, wcol_ref[...], 2 * k)
-        for side in range(2):
-
-            def body(h, carry, side=side):
-                re, im = entries(0, side * (nv // ROWS) + h)
-                top = pl.ds(pl.multiple_of(h * ROWS, ROWS), ROWS)
-                low = pl.ds(pl.multiple_of(nv + h * ROWS, ROWS), ROWS)
-                right[side, k, top, :facet] = re
-                right[side, k, top, facet:] = -im
-                right[side, k, low, :facet] = im
-                right[side, k, low, facet:] = re
-                return carry
-
-            lax.fori_loop(0, nv // ROWS, body, 0)
+
+    def build_columns(side, k):
+        def body(h, carry):
+            re, im = entries(0, side * (nv // ROWS) + h)
+            top = pl.ds(pl.multiple_of(h * ROWS, ROWS), ROWS)
+            low = pl.ds(pl.multiple_of(nv + h * ROWS, ROWS), ROWS)
+            right[side, k, top, :facet] = re
+            right[side, k, top, facet:] = -im
+            right[side, k, low, :facet] = im
+            right[side, k, low, facet:] = re
+            return carry
+
+        lax.fori_loop(0, nv // ROWS, body, 0)
 
     def build_rows(k):
         index = iota((sg // ROWS, facet), 0) * ROWS
@@ -347,7 +347,8 @@
 
     write_fine(0, gcol)
     for k in range(n_sub):
-        build_columns(k)
+        column_phases(k)
+        build_columns(1, k)
         if k == 0:
             for load in loads:
                 load.wait()
@@ -357,6 +358,7 @@
         swap = remote(hsend.at[k], hgot.at[k], isend.at[k], irecv.at[k], partner)
         swap.start()
         swaps.append(swap)
+        build_columns(0, k)
         hown[k] = contract(0, k)
         if k == 0:
             write_fine(1, grow)

time: 36.8 us -> 36.7 us (level)
  no operation moved by 1% of the time
where the time goes in v5:
time: 36.7 us; the launch traced here: 36.5 us
  Pallas kernels  34.9 us (95%)
  local copies, waits for them, and re-layouts  1.57 us (4%)
    pallas_call x1, Pallas kernels, fused_local(): pl.pallas_call(functools.partial(fused_kernel, (n_side, n_z, n_sub, facet...  34.9 us
    unnamed x1, local copies, waits for them, and re-layouts  1.57 us

profile of v5, /device:TPU:0, one launch (start us, length us, event | category | flops | bytes accessed | tf_op | source)
XLA Modules:
  0.0 36.5 jit_solution(11441991397110274708)
XLA Ops:
  0.0 34.9 %shard_map.91 = f32[2,2,64,128]{3,2,1,0:T(8,128)} custom-call(bf16[2,512,512]{2,1,0:T(8,128)(2,1)} %image_hbm.1, f32[1,512]{1,0:T(1,128)} %bitcast.2, f32[1,512]{1,0:T(1,128)} %bitcast.3, f32[2]{0:T(128)} %w_ref.1, s32[8]{0:T(128)} %row_off_ref.1, s32[4]{0:T(128)} %col_off_ref.1, s32[2]{0:T(128)} %band_ref.1, s32[2]{0:T(128)} %sub_off_ref.1, s32[2]{0:T(128)} %sub_col_ref.1), custom_call_target="tpu_custom_call" | custom-call | tf_op jit(solution)/shard_map/pallas_call | solution.py:414
  34.9 1.6 %copy.11 = f32[2,2,64,128]{3,2,1,0:T(8,128)} copy(f32[2,2,64,128]{3,2,1,0:T(8,128)} %shard_map.91) | data formatting | bytes 262144

commit v6 on v5

--- a/solution.py
+++ b/solution.py
@@ -373,7 +373,7 @@
             )
         for ch in range(2 * PARTS * k, 2 * PARTS * (k + 1)):
             emit(ch)
-            if k > 0 and ch == 2 * PARTS * k + 1:
+            if k > 0 and ch >= 2 * PARTS * k + 1:
                 pump()
     while len(copies2) < n_chunk - 1:
         pump()

time: 36.7 us -> 36.7 us (level)
  no operation moved by 1% of the time
where the time goes in v6:
time: 36.7 us; the launch traced here: 36.5 us
  Pallas kernels  34.9 us (95%)
  local copies, waits for them, and re-layouts  1.57 us (4%)
    pallas_call x1, Pallas kernels, fused_local(): pl.pallas_call(functools.partial(fused_kernel, (n_side, n_z, n_sub, facet...  34.9 us
    unnamed x1, local copies, waits for them, and re-layouts  1.57 us

profile of v6, /device:TPU:0, one launch (start us, length us, event | category | flops | bytes accessed | tf_op | source)
XLA Modules:
  0.0 36.5 jit_solution(1648299700507880314)
XLA Ops:
  0.0 34.9 %shard_map.91 = f32[2,2,64,128]{3,2,1,0:T(8,128)} custom-call(bf16[2,512,512]{2,1,0:T(8,128)(2,1)} %image_hbm.1, f32[1,512]{1,0:T(1,128)} %bitcast.2, f32[1,512]{1,0:T(1,128)} %bitcast.3, f32[2]{0:T(128)} %w_ref.1, s32[8]{0:T(128)} %row_off_ref.1, s32[4]{0:T(128)} %col_off_ref.1, s32[2]{0:T(128)} %band_ref.1, s32[2]{0:T(128)} %sub_off_ref.1, s32[2]{0:T(128)} %sub_col_ref.1), custom_call_target="tpu_custom_call" | custom-call | tf_op jit(solution)/shard_map/pallas_call | solution.py:414
  34.9 1.6 %copy.11 = f32[2,2,64,128]{3,2,1,0:T(8,128)} copy(f32[2,2,64,128]{3,2,1,0:T(8,128)} %shard_map.91) | data formatting | bytes 262144
